TPU v7x, 32 devices: a whole 2x2x4 slice. The times are simulated.
32 devices in a mesh: groups: 2 (over y), seq: 4 (over x, core), chan: 4 (over z).
Axes of the slice: x: 2, y: 2, z: 4, core: 2. Of those that a mesh axis runs over, the one named last changes fastest.
Arguments:
- tokens: bfloat16 [4096, 4096], P(('groups', 'seq'), 'chan'), parts along dimension 0, may hold values from -6 to 6
- norm_gain: float32 [4096], replicated, may hold values from 0.5 to 1.5
- proj_weight: bfloat16 [4096, 3, 4096], P('seq', None, 'chan'), may hold values from -0.09375 to 0.09375
- short_filter: float32 [3, 3, 4096], P(None, None, 'chan'), may hold values from -2.5 to 2.5
- long_filter: float32 [4096, 2048], P('chan', 'seq'), may hold values from -4 to 4, as said below
- skip_gain: float32 [4096], P('chan'), may hold values from 0.5 to 1.5
- out_weight: bfloat16 [4096, 4096], P(None, 'chan'), may hold values from -0.09375 to 0.09375
Outputs:
- block_out: bfloat16 [4096, 4096], P(('groups', 'seq'), 'chan'), parts along dimension 0
There are 2 independent parts, one for each index of `groups`. A program takes and returns all parts, laid end to end along the dimension named above; an argument that names none is the same for every part. Nothing has to cross between parts.
Inputs may be any that keep to these rules, and one draw needn't show every extreme that they name: `long_filter`: filter taps of the sequence-long convolution.
All inputs are finite; a program needn't handle non-finite values.
Results may differ from a plain program's by a relative error of at most 0.012.
Values may be sent and summed in bfloat16 or wider, within the bound.
A program may use at most 128 MiB of HBM per device.

v0:
```python
import math
import jax
import jax.numpy as jnp
from jax import lax
from jax.sharding import PartitionSpec as P

SHORT = 3
EPSILON = 1e-06
HIGHEST = lax.Precision.HIGHEST


def from_behind(value, axis, steps):
    count = lax.axis_size(axis)
    initial, last = (max(0, -steps), min(count, count - steps))
    return lax.ppermute(value, axis, [(source, source + steps) for source in range(initial, last)])


def angle_table(row_count, col_count, period, sign):
    row_index = lax.iota(jnp.int32, row_count)[:, None]
    col_index = lax.iota(jnp.int32, col_count)[None, :]
    angles = (row_index * col_index % period).astype(jnp.float32) * (sign * 2.0 * math.pi / period)
    return (jnp.cos(angles), jnp.sin(angles))


def forward_spectrum(signal_rows, first, second):
    channels = signal_rows.shape[0]
    grid_rows = signal_rows.reshape(channels, first, second)
    cos_first, sin_first = angle_table(first, first, first, -1.0)
    part_re = jnp.einsum("cab,ak->ckb", grid_rows, cos_first, precision=HIGHEST)
    part_im = jnp.einsum("cab,ak->ckb", grid_rows, sin_first, precision=HIGHEST)
    twist_cos, twist_sin = angle_table(first, second, first * second, -1.0)
    part_re, part_im = (
        part_re * twist_cos - part_im * twist_sin,
        part_re * twist_sin + part_im * twist_cos,
    )
    cos_second, sin_second = angle_table(second, second, second, -1.0)
    spectrum_real = jnp.einsum("ckb,bm->ckm", part_re, cos_second, precision=HIGHEST) - jnp.einsum(
        "ckb,bm->ckm", part_im, sin_second, precision=HIGHEST
    )
    spec_im = jnp.einsum("ckb,bm->ckm", part_re, sin_second, precision=HIGHEST) + jnp.einsum(
        "ckb,bm->ckm", part_im, cos_second, precision=HIGHEST
    )
    return (spectrum_real, spec_im)


def inverse_spectrum(spectrum_real, spec_im, first, second):
    channels = spectrum_real.shape[0]
    cos_second, sin_second = angle_table(second, second, second, 1.0)
    part_re = jnp.einsum("ckm,bm->ckb", spectrum_real, cos_second, precision=HIGHEST) - jnp.einsum(
        "ckm,bm->ckb", spec_im, sin_second, precision=HIGHEST
    )
    part_im = jnp.einsum("ckm,bm->ckb", spectrum_real, sin_second, precision=HIGHEST) + jnp.einsum(
        "ckm,bm->ckb", spec_im, cos_second, precision=HIGHEST
    )
    twist_cos, twist_sin = angle_table(first, second, first * second, 1.0)
    part_re, part_im = (
        part_re * twist_cos - part_im * twist_sin,
        part_re * twist_sin + part_im * twist_cos,
    )
    cos_first, sin_first = angle_table(first, first, first, 1.0)
    result = jnp.einsum("ckb,ak->cab", part_re, cos_first, precision=HIGHEST) - jnp.einsum(
        "ckb,ak->cab", part_im, sin_first, precision=HIGHEST
    )
    return result.reshape(channels, first * second) / (first * second)


def spectral_conv(signal_rows, filter_rows):
    channels, length = signal_rows.shape
    padded_len = 2 * length
    log_len = padded_len.bit_length() - 1
    first = 1 << log_len // 2
    second = padded_len // first
    zeros_tail = jnp.zeros((channels, length), jnp.float32)
    sig_re, sig_im = forward_spectrum(
        jnp.concatenate([signal_rows, zeros_tail], axis=1), first, second
    )
    tap_re, tap_im = forward_spectrum(
        jnp.concatenate([filter_rows, zeros_tail], axis=1), first, second
    )
    prod_re = sig_re * tap_re - sig_im * tap_im
    prod_im = sig_re * tap_im + sig_im * tap_re
    return inverse_spectrum(prod_re, prod_im, first, second)[:, :length]


def short_filter_output(projected, rim_cells, kernel_coefficients):
    count = kernel_coefficients.shape[0]
    steps_len = projected.shape[2]
    extended = jnp.concatenate([rim_cells, projected], axis=2).astype(jnp.float32)
    total = jnp.zeros(projected.shape, jnp.float32)
    for tap in range(count):
        total = (
            total
            + kernel_coefficients[tap][:, :, None]
            * extended[:, :, count - 1 - tap : count - 1 - tap + steps_len]
        )
    return total.astype(jnp.bfloat16)


def hyena_mixer(keys_rows, values_rows, long_taps, skip_part):
    middle = keys_rows.astype(jnp.float32) * values_rows.astype(jnp.float32)
    return (spectral_conv(middle, long_taps) + skip_part[:, None] * middle).astype(jnp.bfloat16)


def body(tokens, norm_gain, proj_weight, short_filter, long_filter, skip_gain, out_weight):
    seq_count = lax.axis_size("seq")
    local_rows = tokens.shape[0]
    local_chan = proj_weight.shape[2]
    subset = local_chan // seq_count
    length = local_rows * seq_count
    offset = lax.axis_index("seq") * subset
    whole = lax.all_gather(tokens, "chan", axis=1, tiled=True)
    wide = whole.astype(jnp.float32)
    rescaled_signal = (
        wide * lax.rsqrt(jnp.mean(wide * wide, axis=1, keepdims=True) + EPSILON) * norm_gain
    ).astype(jnp.bfloat16)
    projected = lax.dot_general(
        lax.all_gather(proj_weight, "seq", axis=0, tiled=True),
        rescaled_signal,
        (((0,), (1,)), ((), ())),
        preferred_element_type=jnp.float32,
    ).astype(jnp.bfloat16)
    taps_grid = long_filter.reshape(1, seq_count, subset, local_rows)
    long_taps = lax.all_to_all(taps_grid, "seq", split_axis=1, concat_axis=3, tiled=True).reshape(
        subset, length
    )
    skip_part = lax.dynamic_slice_in_dim(skip_gain, offset, subset, 0)
    rim_cells = from_behind(projected[:, :, local_rows - (SHORT - 1) :], "seq", 1)
    featured = short_filter_output(projected, rim_cells, short_filter)
    pair_grid = featured[1:].reshape(2, seq_count, subset, local_rows)
    moved = lax.all_to_all(pair_grid, "seq", split_axis=1, concat_axis=3, tiled=True).reshape(
        2, subset, length
    )
    result = hyena_mixer(moved[0], moved[1], long_taps, skip_part)
    returned = lax.all_to_all(
        result.reshape(1, subset, length), "seq", split_axis=2, concat_axis=0, tiled=True
    )
    returned = returned.reshape(local_chan, local_rows)
    gated = (featured[0].astype(jnp.float32) * returned.astype(jnp.float32)).astype(jnp.bfloat16)
    full_mix = lax.all_gather(gated, "chan", axis=0, tiled=True)
    update = lax.dot_general(
        full_mix, out_weight, (((0,), (0,)), ((), ())), preferred_element_type=jnp.float32
    )
    return (tokens.astype(jnp.float32) + update).astype(jnp.bfloat16)


def solution(mesh):
    placed = (
        P(("groups", "seq"), "chan"),
        P(),
        P("seq", None, "chan"),
        P(None, None, "chan"),
        P("chan", "seq"),
        P("chan"),
        P(None, "chan"),
    )
    return jax.shard_map(
        body, mesh=mesh, in_specs=placed, out_specs=P(("groups", "seq"), "chan"), check_vma=False
    )
```

profile of v0, /device:TPU:0, one launch (start us, length us, event | category | flops | bytes accessed | tf_op | source)
XLA Modules:
  0.0 568.1 jit_solution(13785095065940686060)
XLA Ops:
  6.5 0.7 all-gather.4.cloned.1.call-update
  7.3 0.0 all-gather.6.cloned.1.call-start
  7.3 0.7 all-gather.6.cloned.1.call-update
  8.0 4.2 all-to-all-start.1
  12.3 80.1 %all-gather.4.cloned.1.call-done = bf16[512,4096]{1,0:T(8,128)(2,1)} async-done(((bf16[512,1024]{1,0:T(8,128)(2,1)}), bf16[512,4096]{1,0:T(8,128)(2,1)}) %all-gather.4.cloned.1.call-update) | async-done | bytes 4194320 | tf_op jit(solution)/shard_map/all_gather | solution.py:111
  92.4 3.1 fusion
  95.5 151.8 %all-gather.6.cloned.1.call-done = bf16[4096,3,1024]{2,0,1:T(8,128)(2,1)} async-done(((bf16[1024,3,1024]{2,0,1:T(8,128)(2,1)}), bf16[4096,3,1024]{2,0,1:T(8,128)(2,1)}) %all-gather.6.cloned.1.call-update) | async-done | bytes 25165840 | tf_op jit(solution)/shard_map/all_gather | solution.py:117
  247.3 18.2 %convert_bitcast_fusion = bf16[3,1024,512]{1,2,0:T(8,128)(2,1)S(1)} fusion(bf16[4096,3,1024]{2,0,1:T(8,128)(2,1)} %all-gather.6.cloned.1.call-done, bf16[512,4096]{1,0:T(8,128)(2,1)} %all-gather.4.cloned.1.call-done, f32[4096]{0:T(1024)S(1)} %copy-done.5, f32[512]{0:T(512)S(1)} %add_rsqrt_fusion), kind=kOutput, calls=%fused_computation.53 | convolution fusion | flops 12894863360 | bytes 32524288 | tf_op jit(solution)/shard_map/dot_general | solution.py:116
  265.5 2.2 collective-permute-start
  267.7 0.8 collective-permute-done
  268.5 0.9 maximum_convert_fusion
  269.4 2.1 fusion.4
  271.5 1.6 copy-done.1
  273.1 0.2 slice.55
  273.3 1.5 copy.202
  274.9 4.4 all-to-all-start
  279.3 0.5 all-gather.8.cloned.1.call-start
  279.8 0.1 multiply_cosine_fusion.1
  280.0 0.1 copy.99
  280.0 0.1 multiply_sine_fusion.1
  280.2 0.1 copy.102
  280.3 0.8 dynamic_slice.3
  281.0 0.1 multiply_sine_fusion
  281.2 1.9 copy.108
  283.1 0.3 concatenate.11
  283.4 7.2 %fusion.23 = f32[64,256,64]{1,0,2:T(8,128)} fusion(f32[256,64,64]{0,2,1:T(8,128)S(1)} %bitcast.128), kind=kOutput, calls=%fused_computation.36 | convolution fusion | flops 805363712 | bytes 8388608 | tf_op jit(solution)/shard_map/cab,ak->ckb/dot_general | solution.py:30
  290.6 7.2 %fusion.25 = f32[64,256,64]{1,0,2:T(8,128)} fusion(f32[256,64,64]{0,2,1:T(8,128)S(1)} %bitcast.129), kind=kOutput, calls=%fused_computation.38 | convolution fusion | flops 805363712 | bytes 8388608 | tf_op jit(solution)/shard_map/cab,ak->ckb/dot_general | solution.py:29
  297.7 7.3 %all-to-all-done = bf16[2,4,256,512]{2,3,0,1:T(8,128)(2,1)} async-done(((bf16[2,4,256,512]{2,3,0,1:T(8,128)(2,1)}), bf16[2,4,256,512]{2,3,0,1:T(8,128)(2,1)}, u32[]{:S(2)}, u32[]{:S(2)}) %all-to-all-start) | async-done | bytes 2097184 | tf_op jit(solution)/shard_map/all_to_all | solution.py:130
  305.0 1.7 copy.203
  306.8 0.2 convert_multiply_fusion.3
  307.0 0.3 concatenate.10
  307.3 1.9 copy-done
  309.2 7.1 %fusion.35 = f32[64,256,64]{1,0,2:T(8,128)} fusion(f32[256,64,64]{0,2,1:T(8,128)S(1)} %bitcast.130), kind=kOutput, calls=%fused_computation.48 | convolution fusion | flops 805363712 | bytes 8388608 | tf_op jit(solution)/shard_map/cab,ak->ckb/dot_general | solution.py:30
  316.3 12.5 %subtract_bitcast_fusion = (f32[256,64,64]{0,1,2:T(8,128)S(1)}, f32[256,64,64]{0,1,2:T(8,128)S(1)}, f32[256,64,64]{0,1,2:T(8,128)S(1)}, f32[256,64,64]{0,1,2:T(8,128)S(1)}) fusion(f32[64,256,64]{1,0,2:T(8,128)} %fusion.23, f32[64,256,64]{1,0,2:T(8,128)} %fusion.25, f32[64,64]{0,1:T(8,128)S(1)} %copy.102, f32[64,64]{0,1:T(8,128)S(1)} %copy.99, ...), kind=kOutput, calls=%fused_computation.23 | convolution fusion | flops 817946624 | bytes 33587200 | tf_op jit(solution)/shard_map/cab,ak->ckb/dot_general | solution.py:29
  328.8 6.5 %fusion.15 = f32[256,64,64]{0,2,1:T(8,128)S(1)} fusion(f32[256,64,64]{0,1,2:T(8,128)S(1)} %get-tuple-element.10), kind=kOutput, calls=%fused_computation.28 | convolution fusion | flops 805363712 | bytes 8388608 | tf_op jit(solution)/shard_map/ckb,bm->ckm/dot_general | solution.py:40
  335.3 6.9 %fusion.17 = f32[256,64,64]{0,2,1:T(8,128)S(1)} fusion(f32[256,64,64]{0,1,2:T(8,128)S(1)} %get-tuple-element.10), kind=kOutput, calls=%fused_computation.30 | convolution fusion | flops 805363712 | bytes 8388608 | tf_op jit(solution)/shard_map/ckb,bm->ckm/dot_general | solution.py:37
  342.3 7.3 %fusion.27 = f32[256,64,64]{0,2,1:T(8,128)} fusion(f32[256,64,64]{0,1,2:T(8,128)S(1)} %get-tuple-element.13), kind=kOutput, calls=%fused_computation.40 | convolution fusion | flops 805363712 | bytes 8388608 | tf_op jit(solution)/shard_map/ckb,bm->ckm/dot_general | solution.py:40
  349.6 6.5 %fusion.29 = f32[256,64,64]{0,2,1:T(8,128)S(1)} fusion(f32[256,64,64]{0,1,2:T(8,128)S(1)} %get-tuple-element.13), kind=kOutput, calls=%fused_computation.42 | convolution fusion | flops 805363712 | bytes 8388608 | tf_op jit(solution)/shard_map/ckb,bm->ckm/dot_general | solution.py:37
  356.1 7.3 %fusion.47 = f32[256,64,64]{0,2,1:T(8,128)S(1)} fusion(f32[256,64,64]{0,2,1:T(8,128)S(1)} %fusion.17, f32[256,64,64]{0,1,2:T(8,128)S(1)} %get-tuple-element.9), kind=kOutput, calls=%fused_computation.56 | convolution fusion | flops 806412288 | bytes 12582912 | tf_op jit(solution)/shard_map/ckb,bm->ckm/dot_general | solution.py:37
  363.3 7.4 %fusion.50 = f32[256,64,64]{0,2,1:T(8,128)} fusion(f32[256,64,64]{0,2,1:T(8,128)S(1)} %fusion.15, f32[256,64,64]{0,1,2:T(8,128)S(1)} %get-tuple-element.9), kind=kOutput, calls=%fused_computation.57 | convolution fusion | flops 806412288 | bytes 12582912 | tf_op jit(solution)/shard_map/ckb,bm->ckm/dot_general | solution.py:40
  370.7 7.4 %fusion.41 = f32[256,64,64]{0,2,1:T(8,128)} fusion(f32[256,64,64]{0,2,1:T(8,128)S(1)} %fusion.29, f32[256,64,64]{0,1,2:T(8,128)S(1)} %get-tuple-element.14), kind=kOutput, calls=%fused_computation.54 | convolution fusion | flops 806412288 | bytes 12582912 | tf_op jit(solution)/shard_map/ckb,bm->ckm/dot_general | solution.py:37
  378.1 10.5 %multiply_add_fusion.1 = (f32[256,64,64]{0,2,1:T(8,128)S(1)}, f32[256,64,64]{0,2,1:T(8,128)S(1)}) fusion(f32[256,64,64]{0,2,1:T(8,128)S(1)} %fusion.47, f32[256,64,64]{0,2,1:T(8,128)} %fusion.41, f32[256,64,64]{0,2,1:T(8,128)} %fusion.50, f32[256,64,64]{0,2,1:T(8,128)} %fusion.27, f32[256,64,64]{0,1,2:T(8,128)S(1)} %get-tuple-element.14), kind=kOutput, calls=%fused_computation.20 | convolution fusion | flops 812703744 | bytes 29360128 | tf_op jit(solution)/shard_map/ckb,bm->ckm/dot_general | solution.py:40
  388.6 4.4 fusion.61
  393.0 4.5 fusion.78
  397.4 4.8 convolution_subtract_fusion
  402.2 6.8 %multiply_subtract_fusion = (f32[256,64,64]{0,2,1:T(8,128)S(1)}, f32[256,64,64]{0,2,1:T(8,128)S(1)}) fusion(f32[256,64,64]{0,2,1:T(8,128)S(1)} %convolution_subtract_fusion, f32[64,64]{1,0:T(8,128)S(1)} %get-tuple-element.18, f32[64,64]{1,0:T(8,128)S(1)} %get-tuple-element.19, f32[256,64,64]{0,2,1:T(8,128)S(1)} %fusion.61, ...), kind=kOutput, calls=%fused_computation.19 | convolution fusion | flops 812703744 | bytes 21004288 | tf_op jit(solution)/shard_map/ckm,bm->ckb/dot_general | solution.py:52
  409.0 6.0 %fusion.9 = f32[64,256,64]{1,0,2:T(8,128)S(1)} fusion(f32[256,64,64]{0,2,1:T(8,128)S(1)} %get-tuple-element.8), kind=kOutput, calls=%fused_computation.13 | convolution fusion | flops 805363712 | bytes 8388608 | tf_op jit(solution)/shard_map/ckb,ak->cab/dot_general | solution.py:61
  415.1 6.4 %multiply_bitcast_fusion = f32[256,64,64]{0,1,2:T(8,128)S(1)} fusion(f32[64,256,64]{1,0,2:T(8,128)S(1)} %fusion.9, f32[256,64,64]{0,2,1:T(8,128)S(1)} %get-tuple-element.7), kind=kOutput, calls=%fused_computation.17 | convolution fusion | flops 807460864 | bytes 12582912 | tf_op jit(solution)/shard_map/ckb,ak->cab/dot_general | solution.py:61
  421.4 2.4 copy.127
  423.9 0.4 fusion.57
  424.3 11.7 %copy.204 = bf16[1,256,2048]{1,0,2:T(2,128)(2,1)S(1)} copy(bf16[1,256,2048]{1,2,0:T(8,128)(2,1)S(1)} %fusion.57) | data formatting | bytes 2097152 | tf_op jit(solution)/shard_map/reshape | solution.py:135
  436.0 0.5 broadcast.298
  436.5 10.6 %reduce = bf16[2048,256]{1,0:T(8,128)(2,1)S(1)} reduce(bf16[2048,1,256]{2,1,0:T(2,128)(2,1)S(1)} %bitcast.137, bf16[]{:T(256)} %broadcast.298), dimensions={1}, to_apply=%bitcast.127.reduce_sub_computation | reduce | bytes 2097154
  447.1 0.3 reshape.133
  447.5 17.1 %all_to_all.39 = bf16[4,2,65536]{2,1,0:T(2,128)(2,1)S(1)} all-to-all(bf16[4,2,65536]{2,1,0:T(2,128)(2,1)S(1)} %reshape.133), channel_id=1, replica_groups=mesh['groups'=2,'seq'=4,'chan'=4] {'seq'}, dimensions={0} | all-to-all | bytes 2097152 | tf_op jit(solution)/shard_map/all_to_all | solution.py:134
  464.5 0.9 reshape.134
  465.5 0.2 copy.129
  465.7 0.2 convert_bitcast_fusion.1
  465.9 1.4 copy.130
  467.2 0.5 copy.156
  467.7 2.6 fusion.56
  470.3 0.0 all-gather.8.cloned.1.call-update
  470.3 80.9 %all-gather.8.cloned.1.call-done = bf16[4096,512]{0,1:T(8,128)(2,1)} async-done(((bf16[1024,512]{0,1:T(8,128)(2,1)}), bf16[4096,512]{0,1:T(8,128)(2,1)}) %all-gather.8.cloned.1.call-update) | async-done | bytes 4194320 | tf_op jit(solution)/shard_map/all_gather | solution.py:139
  551.2 10.1 %add_convert_fusion = bf16[512,1024]{1,0:T(8,128)(2,1)} fusion(bf16[512,1024]{1,0:T(8,128)(2,1)S(1)} %copy-done.3, bf16[4096,512]{0,1:T(8,128)(2,1)} %all-gather.8.cloned.1.call-done, bf16[4096,1024]{1,0:T(8,128)(2,1)} %param.13), kind=kOutput, calls=%fused_computation.67 | convolution fusion | flops 4296540160 | bytes 14680064 | tf_op jit(solution)/shard_map/dot_general | solution.py:140
  (15 shorter events, 0.1 us)
Async XLA Ops:
  6.5 85.9 %all-gather.4.cloned.1.call-start = ((), (), s32[]{:S(2)}) async-start(), calls=%async_computation.3 | async-start | bytes 5242880 | tf_op jit(solution)/shard_map/all_gather | solution.py:111
  7.3 240.0 %all-gather.6.cloned.1.call-start = ((), (), s32[]{:S(2)}) async-start(), calls=%async_computation.4 | async-start | bytes 31457280 | tf_op jit(solution)/shard_map/all_gather | solution.py:117
  8.0 239.3 %copy-start.5 = (f32[4096]{0:T(1024)S(1)}, f32[4096]{0:T(1024)}, u32[]{:S(2)}) copy-start(f32[4096]{0:T(1024)} %param.8) | copy-start | bytes 49156
  8.0 266.8 %all-to-all-start.1 = ((f32[1,4,256,512]{3,2,0,1:T(8,128)}), f32[1,4,256,512]{3,2,0,1:T(8,128)S(1)}, u32[]{:S(2)}, u32[]{:S(2)}) async-start(f32[1,4,256,512]{3,2,0,1:T(8,128)} %bitcast.143), calls=%async_computation.1 | async-start | bytes 4194304 | tf_op jit(solution)/shard_map/all_to_all | solution.py:123
  95.5 172.2 %copy-start.4 = (f32[3,3,1024]{2,1,0:T(4,128)S(1)}, f32[3,3,1024]{2,1,0:T(4,128)}, u32[]{:S(2)}) copy-start(f32[3,3,1024]{2,1,0:T(4,128)} %param.10) | copy-start | bytes 110596
  265.5 3.0 collective-permute-start
  271.5 1.6 copy-start.1
  274.8 6.2 %copy-start.2 = (f32[1,4,256,512]{3,2,0,1:T(8,128)}, f32[1,4,256,512]{3,2,0,1:T(8,128)S(1)}, u32[]{:S(2)}) copy-start(f32[1,4,256,512]{3,2,0,1:T(8,128)S(1)} %all-to-all-done.1) | copy-start | bytes 6291460
  274.9 30.2 %all-to-all-start = ((bf16[2,4,256,512]{2,3,0,1:T(8,128)(2,1)}), bf16[2,4,256,512]{2,3,0,1:T(8,128)(2,1)}, u32[]{:S(2)}, u32[]{:S(2)}) async-start(bf16[2,4,256,512]{2,3,0,1:T(8,128)(2,1)} %bitcast.136), calls=%async_computation | async-start | bytes 4194304 | tf_op jit(solution)/shard_map/all_to_all | solution.py:130
  279.3 271.9 %all-gather.8.cloned.1.call-start = ((), (), s32[]{:S(2)}) async-start(), calls=%async_computation.5 | async-start | bytes 5242880 | tf_op jit(solution)/shard_map/all_gather | solution.py:139
  307.3 1.9 copy-start
  467.2 84.0 %copy-start.3 = (bf16[512,1024]{1,0:T(8,128)(2,1)S(1)}, bf16[512,1024]{1,0:T(8,128)(2,1)}, u32[]{:S(2)}) copy-start(bf16[512,1024]{1,0:T(8,128)(2,1)} %param.7) | copy-start | bytes 3145732
Sparse Core Ops, SparseCore 0:
  8.9 83.4 all-gather.3
  94.0 153.2 all-gather.5
  470.5 80.7 all-gather.7
where the time goes:
time: 574 us; the launch traced here: 568 us
  waiting for transfers between devices  322 us (56%)
  matrix products  155 us (27%)
  local copies, waits for them, and re-layouts  28.4 us (5%)
  other arithmetic  20.5 us (4%)
  blocking collectives  17.1 us (3%)
  between operations  13.7 us (2%)
  starting transfers between devices  11.4 us (2%)
    all_gather x1, waiting for transfers between devices, body(): lax.all_gather(proj_weight, 'seq', axis=0, tiled=True)  152 us
    all_gather x1, waiting for transfers between devices, body(): full_mix = lax.all_gather(gated, 'chan', axis=0, tiled=True)  80.9 us
    all_gather x1, waiting for transfers between devices, body(): whole = lax.all_gather(tokens, 'chan', axis=1, tiled=True)  80.1 us
    dot_general x2, matrix products, forward_spectrum(): part_re = jnp.einsum('cab,ak->ckb', grid_rows, cos_first, precision=HIGHEST)  19.7 us
    dot_general x1, matrix products, body(): lax.dot_general(lax.all_gather(proj_weight, 'seq', axis=0, tiled=True), r...  18.2 us
    dot_general x2, matrix products, forward_spectrum(): jnp.einsum('ckb,bm->ckm', part_re, sin_second, precision=HIGHEST)  17.9 us
    all_to_all x1, blocking collectives, body(): lax.all_to_all(result.reshape(1, subset, length), 'seq', split_axis=2, co...  17.1 us
    dot_general x2, matrix products, forward_spectrum(): jnp.einsum('ckb,bm->ckm', part_re, cos_second, precision=HIGHEST)  14.6 us
  transfers between devices with their start and end apart: 6, of which 5 were waited for; matrix products, arithmetic and copies ran while one was open for 8% of the time, Pallas kernels for 0%

commit v1 on v0

--- a/solution.py
+++ b/solution.py
@@ -108,7 +108,8 @@
     subset = local_chan // seq_count
     length = local_rows * seq_count
     offset = lax.axis_index("seq") * subset
-    whole = lax.all_gather(tokens, "chan", axis=1, tiled=True)
+    shards = lax.all_gather(tokens, "chan", axis=0, tiled=False)
+    whole = jnp.concatenate(shards, axis=1)
     wide = whole.astype(jnp.float32)
     rescaled_signal = (
         wide * lax.rsqrt(jnp.mean(wide * wide, axis=1, keepdims=True) + EPSILON) * norm_gain

time: 574 us -> 576 us (level)
  waiting for transfers between devices: 322 us -> 316 us
    all_gather x1, waiting for transfers between devices: 152 us -> 145 us  [body(): lax.all_gather(proj_weight, 'seq', axis=0, tiled=True)]
    unnamed x1 -> x2, other arithmetic: 10.6 us -> 13.8 us
  transfers between devices with their start and end apart: 6 -> 6, of which waited for: 5 -> 5; matrix products, arithmetic and copies ran while one was open for 8% -> 9% of each run, Pallas kernels for 0% -> 0%
where the time goes in v1:
time: 576 us; the launch traced here: 570 us
  waiting for transfers between devices  316 us (55%)
  matrix products  156 us (27%)
  local copies, waits for them, and re-layouts  34 us (6%)
  other arithmetic  21.5 us (4%)
  blocking collectives  17.1 us (3%)
  between operations  13.9 us (2%)
  starting transfers between devices  11.4 us (2%)
    all_gather x1, waiting for transfers between devices, body(): lax.all_gather(proj_weight, 'seq', axis=0, tiled=True)  145 us
    all_gather x1, waiting for transfers between devices, body(): full_mix = lax.all_gather(gated, 'chan', axis=0, tiled=True)  80.9 us
    all_gather x1, waiting for transfers between devices, body(): shards = lax.all_gather(tokens, 'chan', axis=0, tiled=False)  80.1 us
    dot_general x2, matrix products, forward_spectrum(): part_re = jnp.einsum('cab,ak->ckb', grid_rows, cos_first, precision=HIGHEST)  19.7 us
    dot_general x1, matrix products, body(): lax.dot_general(lax.all_gather(proj_weight, 'seq', axis=0, tiled=True), r...  19.4 us
    dot_general x2, matrix products, forward_spectrum(): jnp.einsum('ckb,bm->ckm', part_re, sin_second, precision=HIGHEST)  17.8 us
    all_to_all x1, blocking collectives, body(): lax.all_to_all(result.reshape(1, subset, length), 'seq', split_axis=2, co...  17.1 us
    dot_general x2, matrix products, forward_spectrum(): jnp.einsum('ckb,bm->ckm', part_re, cos_second, precision=HIGHEST)  14.8 us
  transfers between devices with their start and end apart: 6, of which 5 were waited for; matrix products, arithmetic and copies ran while one was open for 9% of the time, Pallas kernels for 0%

profile of v1, /device:TPU:0, one launch (start us, length us, event | category | flops | bytes accessed | tf_op | source)
XLA Modules:
  0.0 569.6 jit_solution(14978163512061516414)
XLA Ops:
  6.5 0.7 all-gather.9.cloned.1.call-update
  7.3 0.7 all-gather.5.cloned.1.call-update
  8.0 4.2 all-to-all-start.1
  12.3 80.1 %all-gather.9.cloned.1.call-done = bf16[2048,1024]{1,0:T(8,128)(2,1)} async-done(((bf16[512,1024]{1,0:T(8,128)(2,1)}), bf16[2048,1024]{1,0:T(8,128)(2,1)}) %all-gather.9.cloned.1.call-update) | async-done | bytes 4194320 | tf_op jit(solution)/shard_map/all_gather | solution.py:111
  92.4 3.2 convert_bitcast_fusion
  95.6 5.6 copy.160
  101.2 0.9 fusion
  102.1 145.2 %all-gather.5.cloned.1.call-done = bf16[4096,3,1024]{2,0,1:T(8,128)(2,1)} async-done(((bf16[1024,3,1024]{2,0,1:T(8,128)(2,1)}), bf16[4096,3,1024]{2,0,1:T(8,128)(2,1)}) %all-gather.5.cloned.1.call-update) | async-done | bytes 25165840 | tf_op jit(solution)/shard_map/all_gather | solution.py:118
  247.3 19.4 %convert_bitcast_fusion.1 = bf16[3,1024,512]{1,2,0:T(8,128)(2,1)S(1)} fusion(bf16[4096,3,1024]{2,0,1:T(8,128)(2,1)} %all-gather.5.cloned.1.call-done, f32[512,4096]{1,0:T(8,128)} %bitcast.144, f32[4096]{0:T(1024)S(1)} %copy-done.6, f32[512]{0:T(512)S(1)} %add_rsqrt_fusion), kind=kOutput, calls=%fused_computation.52 | convolution fusion | flops 12892766208 | bytes 36718592 | tf_op jit(solution)/shard_map/dot_general | solution.py:117
  266.7 2.2 collective-permute-start
  268.9 0.8 collective-permute-done
  269.7 0.9 maximum_convert_fusion
  270.6 2.1 fusion.2
  272.7 1.6 copy-done.2
  274.3 0.2 slice.55
  274.5 1.5 copy.207
  276.0 4.4 all-to-all-start
  280.5 0.5 all-gather.7.cloned.1.call-start
  281.0 0.1 multiply_cosine_fusion.1
  281.2 0.1 copy.103
  281.2 0.1 multiply_sine_fusion.1
  281.4 0.1 copy.106
  281.5 0.8 dynamic_slice.3
  282.2 0.1 multiply_sine_fusion
  282.4 1.9 copy.112
  284.3 0.3 concatenate.11
  284.6 7.2 %fusion.21 = f32[64,256,64]{1,0,2:T(8,128)} fusion(f32[256,64,64]{0,2,1:T(8,128)S(1)} %bitcast.135), kind=kOutput, calls=%fused_computation.35 | convolution fusion | flops 805363712 | bytes 8388608 | tf_op jit(solution)/shard_map/cab,ak->ckb/dot_general | solution.py:30
  291.8 7.2 %fusion.23 = f32[64,256,64]{1,0,2:T(8,128)} fusion(f32[256,64,64]{0,2,1:T(8,128)S(1)} %bitcast.136), kind=kOutput, calls=%fused_computation.37 | convolution fusion | flops 805363712 | bytes 8388608 | tf_op jit(solution)/shard_map/cab,ak->ckb/dot_general | solution.py:29
  298.9 7.3 %all-to-all-done = bf16[2,4,256,512]{2,3,0,1:T(8,128)(2,1)} async-done(((bf16[2,4,256,512]{2,3,0,1:T(8,128)(2,1)}), bf16[2,4,256,512]{2,3,0,1:T(8,128)(2,1)}, u32[]{:S(2)}, u32[]{:S(2)}) %all-to-all-start) | async-done | bytes 2097184 | tf_op jit(solution)/shard_map/all_to_all | solution.py:131
  306.2 1.7 copy.208
  308.0 0.2 convert_multiply_fusion.2
  308.2 0.3 concatenate.10
  308.5 1.9 copy-done
  310.4 7.1 %fusion.33 = f32[64,256,64]{1,0,2:T(8,128)} fusion(f32[256,64,64]{0,2,1:T(8,128)S(1)} %bitcast.137), kind=kOutput, calls=%fused_computation.47 | convolution fusion | flops 805363712 | bytes 8388608 | tf_op jit(solution)/shard_map/cab,ak->ckb/dot_general | solution.py:30
  317.5 12.5 %subtract_bitcast_fusion = (f32[256,64,64]{0,1,2:T(8,128)S(1)}, f32[256,64,64]{0,1,2:T(8,128)S(1)}, f32[256,64,64]{0,1,2:T(8,128)S(1)}, f32[256,64,64]{0,1,2:T(8,128)S(1)}) fusion(f32[64,256,64]{1,0,2:T(8,128)} %fusion.21, f32[64,256,64]{1,0,2:T(8,128)} %fusion.23, f32[64,64]{0,1:T(8,128)S(1)} %copy.106, f32[64,64]{0,1:T(8,128)S(1)} %copy.103, ...), kind=kOutput, calls=%fused_computation.22 | convolution fusion | flops 817946624 | bytes 33587200 | tf_op jit(solution)/shard_map/cab,ak->ckb/dot_general | solution.py:29
  330.0 6.5 %fusion.13 = f32[256,64,64]{0,2,1:T(8,128)S(1)} fusion(f32[256,64,64]{0,1,2:T(8,128)S(1)} %get-tuple-element.10), kind=kOutput, calls=%fused_computation.27 | convolution fusion | flops 805363712 | bytes 8388608 | tf_op jit(solution)/shard_map/ckb,bm->ckm/dot_general | solution.py:40
  336.6 6.9 %fusion.15 = f32[256,64,64]{0,2,1:T(8,128)S(1)} fusion(f32[256,64,64]{0,1,2:T(8,128)S(1)} %get-tuple-element.10), kind=kOutput, calls=%fused_computation.29 | convolution fusion | flops 805363712 | bytes 8388608 | tf_op jit(solution)/shard_map/ckb,bm->ckm/dot_general | solution.py:37
  343.5 6.5 %fusion.27 = f32[256,64,64]{0,2,1:T(8,128)S(1)} fusion(f32[256,64,64]{0,1,2:T(8,128)S(1)} %get-tuple-element.13), kind=kOutput, calls=%fused_computation.41 | convolution fusion | flops 805363712 | bytes 8388608 | tf_op jit(solution)/shard_map/ckb,bm->ckm/dot_general | solution.py:37
  350.0 7.4 %fusion.25 = f32[256,64,64]{0,2,1:T(8,128)} fusion(f32[256,64,64]{0,1,2:T(8,128)S(1)} %get-tuple-element.13), kind=kOutput, calls=%fused_computation.39 | convolution fusion | flops 805363712 | bytes 8388608 | tf_op jit(solution)/shard_map/ckb,bm->ckm/dot_general | solution.py:40
  357.4 7.1 %fusion.48 = f32[256,64,64]{0,2,1:T(8,128)S(1)} fusion(f32[256,64,64]{0,2,1:T(8,128)S(1)} %fusion.13, f32[256,64,64]{0,1,2:T(8,128)S(1)} %get-tuple-element.9), kind=kOutput, calls=%fused_computation.56 | convolution fusion | flops 806412288 | bytes 12582912 | tf_op jit(solution)/shard_map/ckb,bm->ckm/dot_general | solution.py:40
  364.5 7.4 %fusion.45 = f32[256,64,64]{0,2,1:T(8,128)} fusion(f32[256,64,64]{0,2,1:T(8,128)S(1)} %fusion.15, f32[256,64,64]{0,1,2:T(8,128)S(1)} %get-tuple-element.9), kind=kOutput, calls=%fused_computation.55 | convolution fusion | flops 806412288 | bytes 12582912 | tf_op jit(solution)/shard_map/ckb,bm->ckm/dot_general | solution.py:37
  371.9 7.4 %fusion.39 = f32[256,64,64]{0,2,1:T(8,128)} fusion(f32[256,64,64]{0,2,1:T(8,128)S(1)} %fusion.27, f32[256,64,64]{0,1,2:T(8,128)S(1)} %get-tuple-element.14), kind=kOutput, calls=%fused_computation.53 | convolution fusion | flops 806412288 | bytes 12582912 | tf_op jit(solution)/shard_map/ckb,bm->ckm/dot_general | solution.py:37
  379.3 10.7 %multiply_add_fusion.1 = (f32[256,64,64]{0,2,1:T(8,128)S(1)}, f32[256,64,64]{0,2,1:T(8,128)S(1)}) fusion(f32[256,64,64]{0,2,1:T(8,128)} %fusion.45, f32[256,64,64]{0,2,1:T(8,128)} %fusion.39, f32[256,64,64]{0,2,1:T(8,128)S(1)} %fusion.48, f32[256,64,64]{0,2,1:T(8,128)} %fusion.25, f32[256,64,64]{0,1,2:T(8,128)S(1)} %get-tuple-element.14), kind=kOutput, calls=%fused_computation.19 | convolution fusion | flops 812703744 | bytes 29360128 | tf_op jit(solution)/shard_map/ckb,bm->ckm/dot_general | solution.py:40
  390.0 4.5 fusion.76
  394.5 4.4 fusion.59
  398.8 4.6 convolution_subtract_fusion
  403.4 6.8 %multiply_subtract_fusion = (f32[256,64,64]{0,2,1:T(8,128)S(1)}, f32[256,64,64]{0,2,1:T(8,128)S(1)}) fusion(f32[256,64,64]{0,2,1:T(8,128)S(1)} %convolution_subtract_fusion, f32[64,64]{1,0:T(8,128)S(1)} %get-tuple-element.18, f32[64,64]{1,0:T(8,128)S(1)} %get-tuple-element.19, f32[256,64,64]{0,2,1:T(8,128)S(1)} %fusion.59, ...), kind=kOutput, calls=%fused_computation.18 | convolution fusion | flops 812703744 | bytes 21004288 | tf_op jit(solution)/shard_map/ckm,bm->ckb/dot_general | solution.py:52
  410.2 6.0 %fusion.7 = f32[64,256,64]{1,0,2:T(8,128)S(1)} fusion(f32[256,64,64]{0,2,1:T(8,128)S(1)} %get-tuple-element.8), kind=kOutput, calls=%fused_computation.12 | convolution fusion | flops 805363712 | bytes 8388608 | tf_op jit(solution)/shard_map/ckb,ak->cab/dot_general | solution.py:61
  416.2 6.4 %multiply_bitcast_fusion = f32[256,64,64]{0,1,2:T(8,128)S(1)} fusion(f32[64,256,64]{1,0,2:T(8,128)S(1)} %fusion.7, f32[256,64,64]{0,2,1:T(8,128)S(1)} %get-tuple-element.7), kind=kOutput, calls=%fused_computation.16 | convolution fusion | flops 807460864 | bytes 12582912 | tf_op jit(solution)/shard_map/ckb,ak->cab/dot_general | solution.py:61
  422.6 2.4 copy.131
  425.1 0.4 fusion.55
  425.5 11.7 %copy.209 = bf16[1,256,2048]{1,0,2:T(2,128)(2,1)S(1)} copy(bf16[1,256,2048]{1,2,0:T(8,128)(2,1)S(1)} %fusion.55) | data formatting | bytes 2097152 | tf_op jit(solution)/shard_map/reshape | solution.py:136
  437.2 0.5 broadcast.298
  437.7 10.6 %reduce.2 = bf16[2048,256]{1,0:T(8,128)(2,1)S(1)} reduce(bf16[2048,1,256]{2,1,0:T(2,128)(2,1)S(1)} %bitcast.146, bf16[]{:T(256)} %broadcast.298), dimensions={1}, to_apply=%bitcast.134.reduce_sub_computation | reduce | bytes 2097154
  448.3 0.3 reshape.141
  448.7 17.1 %all_to_all.39 = bf16[4,2,65536]{2,1,0:T(2,128)(2,1)S(1)} all-to-all(bf16[4,2,65536]{2,1,0:T(2,128)(2,1)S(1)} %reshape.141), channel_id=1, replica_groups=mesh['groups'=2,'seq'=4,'chan'=4] {'seq'}, dimensions={0} | all-to-all | bytes 2097152 | tf_op jit(solution)/shard_map/all_to_all | solution.py:135
  465.8 0.9 reshape.142
  466.7 0.2 copy.133
  466.9 0.2 convert_bitcast_fusion.2
  467.1 1.4 copy.134
  468.5 0.5 copy.161
  469.0 2.6 fusion.54
  471.6 80.9 %all-gather.7.cloned.1.call-done = bf16[4096,512]{0,1:T(8,128)(2,1)} async-done(((bf16[1024,512]{0,1:T(8,128)(2,1)}), bf16[4096,512]{0,1:T(8,128)(2,1)}) %all-gather.7.cloned.1.call-update) | async-done | bytes 4194320 | tf_op jit(solution)/shard_map/all_gather | solution.py:140
  552.5 10.1 %add_convert_fusion = bf16[512,1024]{1,0:T(8,128)(2,1)} fusion(bf16[512,1024]{1,0:T(8,128)(2,1)S(1)} %copy-done.4, bf16[4096,512]{0,1:T(8,128)(2,1)} %all-gather.7.cloned.1.call-done, bf16[4096,1024]{1,0:T(8,128)(2,1)} %param.13), kind=kOutput, calls=%fused_computation.66 | convolution fusion | flops 4296540160 | bytes 14680064 | tf_op jit(solution)/shard_map/dot_general | solution.py:141
  (19 shorter events, 0.1 us)
Async XLA Ops:
  6.5 85.9 %all-gather.9.cloned.1.call-start = ((), (), s32[]{:S(2)}) async-start(), calls=%async_computation.5 | async-start | bytes 5242880 | tf_op jit(solution)/shard_map/all_gather | solution.py:111
  7.3 240.0 %all-gather.5.cloned.1.call-start = ((), (), s32[]{:S(2)}) async-start(), calls=%async_computation.3 | async-start | bytes 31457280 | tf_op jit(solution)/shard_map/all_gather | solution.py:118
  8.0 268.0 %all-to-all-start.1 = ((f32[1,4,256,512]{3,2,0,1:T(8,128)}), f32[1,4,256,512]{3,2,0,1:T(8,128)S(1)}, u32[]{:S(2)}, u32[]{:S(2)}) async-start(f32[1,4,256,512]{3,2,0,1:T(8,128)} %bitcast.152), calls=%async_computation.1 | async-start | bytes 4194304 | tf_op jit(solution)/shard_map/all_to_all | solution.py:124
  95.6 5.6 copy-start.1
  101.2 146.1 %copy-start.6 = (f32[4096]{0:T(1024)S(1)}, f32[4096]{0:T(1024)}, u32[]{:S(2)}) copy-start(f32[4096]{0:T(1024)} %param.8) | copy-start | bytes 49156
  247.3 21.6 %copy-start.5 = (f32[3,3,1024]{2,1,0:T(4,128)S(1)}, f32[3,3,1024]{2,1,0:T(4,128)}, u32[]{:S(2)}) copy-start(f32[3,3,1024]{2,1,0:T(4,128)} %param.10) | copy-start | bytes 110596
  266.7 3.0 collective-permute-start
  272.7 1.7 copy-start.2
  276.0 6.2 %copy-start.3 = (f32[1,4,256,512]{3,2,0,1:T(8,128)}, f32[1,4,256,512]{3,2,0,1:T(8,128)S(1)}, u32[]{:S(2)}) copy-start(f32[1,4,256,512]{3,2,0,1:T(8,128)S(1)} %all-to-all-done.1) | copy-start | bytes 6291460
  276.0 30.2 %all-to-all-start = ((bf16[2,4,256,512]{2,3,0,1:T(8,128)(2,1)}), bf16[2,4,256,512]{2,3,0,1:T(8,128)(2,1)}, u32[]{:S(2)}, u32[]{:S(2)}) async-start(bf16[2,4,256,512]{2,3,0,1:T(8,128)(2,1)} %bitcast.145), calls=%async_computation | async-start | bytes 4194304 | tf_op jit(solution)/shard_map/all_to_all | solution.py:131
  280.5 272.0 %all-gather.7.cloned.1.call-start = ((), (), s32[]{:S(2)}) async-start(), calls=%async_computation.4 | async-start | bytes 5242880 | tf_op jit(solution)/shard_map/all_gather | solution.py:140
  308.5 1.9 copy-start
  468.5 84.0 %copy-start.4 = (bf16[512,1024]{1,0:T(8,128)(2,1)S(1)}, bf16[512,1024]{1,0:T(8,128)(2,1)}, u32[]{:S(2)}) copy-start(bf16[512,1024]{1,0:T(8,128)(2,1)} %param.7) | copy-start | bytes 3145732
Sparse Core Ops, SparseCore 0:
  8.9 83.4 all-gather.8
  94.0 153.2 all-gather.4
  471.7 80.7 all-gather.6
